TPU v7x, 32 devices: a whole 2x2x4 slice. The times are simulated.
32 devices in a mesh: pipe: 4 (over z), tensor: 4 (over x, core), dp: 2 (over y).
Axes of the slice: x: 2, y: 2, z: 4, core: 2. Of those that a mesh axis runs over, the one named last changes fastest.
Arguments:
- inputs: bfloat16 [2, 128, 4096], P(None, ('tensor', 'dp')), may hold values from -6 to 6
- weights: bfloat16 [2, 4, 4096, 4096], P(None, 'pipe', None, 'tensor'), may hold values from -0.09375 to 0.09375
- norm_gains: float32 [2, 4, 4096], P(None, 'pipe'), may hold values from 0.1 to 1.9
- cotangent: bfloat16 [2, 128, 4096], P(None, ('tensor', 'dp')), may hold values from -6 to 6
Outputs:
- act_factor: bfloat16 [4096, 2, 4, 4096], P(('tensor', 'dp'), None, 'pipe')
- grad_factor: bfloat16 [4096, 2, 4, 4096], P(('tensor', 'dp'), None, 'pipe')
All inputs are finite; a program needn't handle non-finite values.
Results may differ from a plain program's by a relative error of at most 0.025.
Values may be sent and summed in bfloat16 or wider, within the bound.
A program may use at most 192 MiB of HBM per device.

v0:
```python
import jax
import jax.numpy as jnp
from jax import lax
from jax.sharding import PartitionSpec as P

EPSILON = 1e-05


def passed_along(array, axis, by):
    peers = lax.axis_size(axis)
    return lax.ppermute(array, axis, [(i, (i + by) % peers) for i in range(peers)])


def normalize(hidden, gain_row):
    hidden_wide = hidden.astype(jnp.float32)
    inverse_rms = lax.rsqrt(jnp.mean(hidden_wide * hidden_wide, axis=-1, keepdims=True) + EPSILON)
    normed = (hidden_wide * inverse_rms * gain_row).astype(jnp.bfloat16)
    return (hidden_wide, inverse_rms, normed)


def rounded(values):
    return lax.optimization_barrier(values.astype(jnp.bfloat16)).astype(jnp.float32)


def body(inputs, weights, norm_gains, cotangent):
    micro_count, shard_rows, features = inputs.shape
    slot_count = weights.shape[0]
    quarter = weights.shape[3]
    tensor_count = lax.axis_size("tensor")
    pipe_count = lax.axis_size("pipe")
    dp_count = lax.axis_size("dp")
    layer_count = slot_count * pipe_count
    section_index = lax.axis_index("pipe")
    column = lax.axis_index("tensor")
    tick_count = micro_count + layer_count - 1
    group_rows = tensor_count * shard_rows
    group_size = micro_count * group_rows
    stash_count = slot_count * micro_count + 1
    own_rows = quarter // dp_count
    inv_tokens = 1.0 / (micro_count * group_rows * dp_count)
    row_base = column * quarter
    normed_stash = jnp.zeros((stash_count, group_rows, features), jnp.bfloat16)
    hidden_stash = jnp.zeros((stash_count, shard_rows, features), jnp.bfloat16)
    grad_stash = jnp.zeros((stash_count, group_rows, features), jnp.bfloat16)
    received = jnp.zeros((shard_rows, features), jnp.bfloat16)
    for moment in range(tick_count):
        micro_index = (moment - section_index) % pipe_count
        layer_index = moment - micro_index
        usable = (micro_index < micro_count) & (layer_index >= 0) & (layer_index < layer_count)
        slot_index = jnp.clip(layer_index // pipe_count, 0, slot_count - 1)
        target = jnp.where(usable, slot_index * micro_count + micro_index, stash_count - 1)
        if moment < micro_count:
            current = jnp.where(section_index == 0, inputs[moment], received)
        else:
            current = received
        weight = lax.dynamic_index_in_dim(weights, slot_index, 0, keepdims=False)[0]
        gain_row = lax.dynamic_index_in_dim(norm_gains, slot_index, 0, keepdims=False)[0]
        hidden_wide, inverse_rms, normed = normalize(current, gain_row)
        gathered = lax.all_gather(normed, "tensor", axis=0, tiled=True)
        normed_stash = lax.dynamic_update_index_in_dim(normed_stash, gathered, target, 0)
        hidden_stash = lax.dynamic_update_index_in_dim(hidden_stash, current, target, 0)
        if moment + 1 < tick_count:
            active = usable & (layer_index + 1 < layer_count)
            product = lax.cond(
                active,
                lambda: jnp.dot(gathered, weight, preferred_element_type=jnp.float32).astype(
                    jnp.bfloat16
                ),
                lambda: jnp.zeros((group_rows, quarter), jnp.bfloat16),
            )
            returned = lax.all_to_all(product, "tensor", split_axis=0, concat_axis=1, tiled=True)
            following = (hidden_wide + returned.astype(jnp.float32)).astype(jnp.bfloat16)
            received = passed_along(following, "pipe", 1)
    act_tokens = normed_stash[: stash_count - 1].reshape(slot_count, group_size, features)
    received = jnp.zeros((shard_rows, features), jnp.bfloat16)
    for moment in range(tick_count):
        micro_index = (section_index + 1 - layer_count + moment) % pipe_count
        depth = moment - micro_index
        layer_index = layer_count - 1 - depth
        usable = (micro_index < micro_count) & (depth >= 0) & (depth < layer_count)
        slot_index = jnp.clip(layer_index // pipe_count, 0, slot_count - 1)
        target = jnp.where(usable, slot_index * micro_count + micro_index, stash_count - 1)
        if moment < micro_count:
            current = jnp.where(section_index == pipe_count - 1, cotangent[moment], received)
        else:
            current = received
        gathered = lax.all_gather(current, "tensor", axis=0, tiled=True)
        grad_stash = lax.dynamic_update_index_in_dim(grad_stash, gathered, target, 0)
        if moment + 1 < tick_count:
            active = usable & (layer_index > 0)
            weight = lax.dynamic_index_in_dim(weights, slot_index, 0, keepdims=False)[0]
            gain_row = lax.dynamic_index_in_dim(norm_gains, slot_index, 0, keepdims=False)[0]
            own_columns = lax.dynamic_slice_in_dim(gathered, row_base, quarter, 1)

            def partial_rows(
                row_start, row_total, own_columns=own_columns, weight=weight, active=active
            ):
                piece = own_columns
                return lax.cond(
                    active,
                    lambda: lax.dot_general(
                        piece, weight, (((1,), (1,)), ((), ())), preferred_element_type=jnp.float32
                    ),
                    lambda: jnp.zeros((row_total, features), jnp.float32),
                )

            back_sum = lax.psum_scatter(
                partial_rows(jnp.int32(0), shard_rows * lax.axis_size("tensor")).astype(
                    jnp.bfloat16
                ),
                "tensor",
                scatter_dimension=0,
                tiled=True,
            ).astype(jnp.float32)
            stored = lax.dynamic_index_in_dim(hidden_stash, target, 0, keepdims=False)
            hidden_wide = stored.astype(jnp.float32)
            inverse_rms = lax.rsqrt(
                jnp.mean(hidden_wide * hidden_wide, axis=-1, keepdims=True) + EPSILON
            )
            scaled = gain_row * back_sum
            inner = jnp.mean(hidden_wide * scaled, axis=-1, keepdims=True)
            following = (
                current.astype(jnp.float32)
                + inverse_rms * scaled
                - inverse_rms**3 * hidden_wide * inner
            ).astype(jnp.bfloat16)
            received = passed_along(following, "pipe", -1)
    grad_tokens = grad_stash[: stash_count - 1].reshape(slot_count, group_size, features)
    own_base = (column * dp_count + lax.axis_index("dp")) * own_rows
    empty = jnp.zeros((own_rows, slot_count, 1, features), jnp.float32)
    pieces = (
        lax.all_gather(act_tokens, "dp", axis=1, tiled=True),
        lax.all_gather(grad_tokens, "dp", axis=1, tiled=True),
    )

    def one_group(group_pick, totals):
        updated = []
        for factor_pick in range(2):
            tokens_block = lax.dynamic_slice_in_dim(
                pieces[factor_pick], group_pick * group_size, group_size, 1
            )
            partials = []
            for slot_pick in range(slot_count):
                tokens_one = tokens_block[slot_pick]
                columns = lax.dynamic_slice_in_dim(tokens_one, own_base, own_rows, 1)
                gram = lax.dot_general(
                    columns,
                    tokens_one,
                    (((0,), (0,)), ((), ())),
                    preferred_element_type=jnp.float32,
                )
                partials.append(rounded(gram * inv_tokens))
            updated.append(totals[factor_pick] + jnp.stack(partials, 1)[:, :, None, :])
        return (updated[0], updated[1])

    act_total, grad_total = lax.fori_loop(
        0, pieces[0].shape[1] // group_size, one_group, (empty, empty)
    )
    act_factor = act_total.astype(jnp.bfloat16)
    grad_factor = grad_total.astype(jnp.bfloat16)
    return (act_factor, grad_factor)


def solution(mesh):
    in_specs = (
        P(None, ("tensor", "dp"), None),
        P(None, "pipe", None, "tensor"),
        P(None, "pipe", None),
        P(None, ("tensor", "dp"), None),
    )
    out_specs = (P(("tensor", "dp"), None, "pipe", None), P(("tensor", "dp"), None, "pipe", None))
    return jax.shard_map(body, mesh=mesh, in_specs=in_specs, out_specs=out_specs, check_vma=False)
```

profile of v0, /device:TPU:0, one launch (start us, length us, event | category | flops | bytes accessed | tf_op | source)
XLA Modules:
  0.0 747.0 jit_solution(15114251936575644437)
XLA Ops:
  12.7 8.6 %all_gather.60 = bf16[64,4096]{1,0:T(8,128)(2,1)S(1)} all-gather(bf16[16,4096]{1,0:T(8,128)(2,1)S(1)} %fusion.157), channel_id=1, replica_groups=mesh['pipe'=4,'tensor'=4,'dp'=2] {'tensor'}, dimensions={0}, use_global_device_ids=true | all-gather | bytes 655360 | tf_op jit(solution)/shard_map/all_gather | solution.py:59
  35.2 6.6 collective-permute-done
  42.1 7.0 all_gather.61
  54.2 7.0 all_to_all.104
  61.4 6.7 collective-permute-done.1
  68.4 7.0 all_gather.62
  75.4 7.0 all_to_all.105
  89.5 7.0 all_gather.63
  96.5 7.1 all_to_all.106
  105.5 6.1 collective-permute-done.3
  111.9 7.0 all_gather.64
  118.8 5.8 conditional.20
  118.8 5.8 fusion.46
  132.7 7.0 all-gather
  141.3 7.7 %all_gather.65 = bf16[64,4096]{1,0:T(8,128)(2,1)} all-gather(bf16[16,4096]{1,0:T(8,128)(2,1)S(1)} %fusion.145), channel_id=1, replica_groups=mesh['pipe'=4,'tensor'=4,'dp'=2] {'tensor'}, dimensions={0}, use_global_device_ids=true | all-gather | bytes 655360 | tf_op jit(solution)/shard_map/all_gather | solution.py:59
  149.0 5.8 conditional.21
  149.0 5.8 fusion.56
  162.9 7.9 %collective-permute-done.5 = bf16[16,4096]{1,0:T(8,128)(2,1)S(1)} collective-permute-done((bf16[16,4096]{1,0:T(8,128)(2,1)S(1)}, bf16[16,4096]{1,0:T(8,128)(2,1)S(1)}, u32[]{:S(2)}, u32[]{:S(2)}) %collective-permute-start.5) | collective-permute-done | bytes 131104 | tf_op jit(solution)/shard_map/ppermute | solution.py:11
  171.0 7.0 all_gather.66
  193.7 7.0 all_gather.67
  219.2 6.3 collective-permute-start.8
  228.0 7.0 all_gather.71
  238.5 26.8 %reduce-scatter.11.cloned.1.call-done = bf16[16,4096]{1,0:T(8,128)(2,1)} async-done(((bf16[64,4096]{1,0:T(8,128)(2,1)}), bf16[16,4096]{1,0:T(8,128)(2,1)}) %reduce-scatter.11.cloned.1.call-update) | async-done | bytes 131088 | tf_op jit(solution)/shard_map/reduce_scatter | solution.py:107
  274.4 7.3 all_gather.72
  285.7 23.5 %reduce-scatter.13.cloned.1.call-done = bf16[16,4096]{1,0:T(8,128)(2,1)} async-done(((bf16[64,4096]{1,0:T(8,128)(2,1)}), bf16[16,4096]{1,0:T(8,128)(2,1)}) %reduce-scatter.13.cloned.1.call-update) | async-done | bytes 131088 | tf_op jit(solution)/shard_map/reduce_scatter | solution.py:107
  317.3 6.9 all_gather.73
  324.3 6.9 conditional.27
  324.3 6.9 fusion.95
  334.4 16.6 %reduce-scatter.15.cloned.1.call-done = bf16[16,4096]{1,0:T(8,128)(2,1)} async-done(((bf16[64,4096]{1,0:T(8,128)(2,1)}), bf16[16,4096]{1,0:T(8,128)(2,1)}) %reduce-scatter.15.cloned.1.call-update) | async-done | bytes 131088 | tf_op jit(solution)/shard_map/reduce_scatter | solution.py:107
  359.1 6.9 all_gather.74
  366.0 6.9 conditional.28
  366.0 6.9 fusion.100
  376.1 20.3 %reduce-scatter.17.cloned.1.call-done = bf16[16,4096]{1,0:T(8,128)(2,1)} async-done(((bf16[64,4096]{1,0:T(8,128)(2,1)}), bf16[16,4096]{1,0:T(8,128)(2,1)}) %reduce-scatter.17.cloned.1.call-update) | async-done | bytes 131088 | tf_op jit(solution)/shard_map/reduce_scatter | solution.py:107
  404.5 6.9 all_gather.75
  415.5 26.3 %reduce-scatter.19.cloned.1.call-done = bf16[16,4096]{1,0:T(8,128)(2,1)} async-done(((bf16[64,4096]{1,0:T(8,128)(2,1)}), bf16[16,4096]{1,0:T(8,128)(2,1)}) %reduce-scatter.19.cloned.1.call-update) | async-done | bytes 131088 | tf_op jit(solution)/shard_map/reduce_scatter | solution.py:107
  450.5 6.9 all_gather.76
  459.3 25.9 %reduce-scatter.21.cloned.1.call-done = bf16[16,4096]{1,0:T(8,128)(2,1)} async-done(((bf16[64,4096]{1,0:T(8,128)(2,1)}), bf16[16,4096]{1,0:T(8,128)(2,1)}) %reduce-scatter.21.cloned.1.call-update) | async-done | bytes 131088 | tf_op jit(solution)/shard_map/reduce_scatter | solution.py:107
  490.8 6.9 all_gather.68
  497.8 7.7 %all_gather.77 = bf16[64,4096]{1,0:T(8,128)(2,1)} all-gather(bf16[16,4096]{1,0:T(8,128)(2,1)S(1)} %collective-permute-done.14), channel_id=1, replica_groups=mesh['pipe'=4,'tensor'=4,'dp'=2] {'tensor'}, dimensions={0}, use_global_device_ids=true | all-gather | bytes 655360 | tf_op jit(solution)/shard_map/all_gather | solution.py:87
  519.3 11.0 %reduce-scatter.23.cloned.1.call-done = bf16[16,4096]{1,0:T(8,128)(2,1)} async-done(((bf16[64,4096]{1,0:T(8,128)(2,1)}), bf16[16,4096]{1,0:T(8,128)(2,1)}) %reduce-scatter.23.cloned.1.call-update) | async-done | bytes 131088 | tf_op jit(solution)/shard_map/reduce_scatter | solution.py:107
  538.4 6.5 all_gather.78
  546.4 25.0 %all-gather.4.cloned.1.call-done = bf16[2,256,4096]{2,1,0:T(8,128)(2,1)} async-done(((bf16[2,128,4096]{2,1,0:T(8,128)(2,1)}), bf16[2,256,4096]{2,1,0:T(8,128)(2,1)}) %all-gather.4.cloned.1.call-update) | async-done | bytes 4194320 | tf_op jit(solution)/shard_map/all_gather | solution.py:132
  571.5 58.6 %all-gather.6.cloned.1.call-done = bf16[2,256,4096]{2,1,0:T(8,128)(2,1)} async-done(((bf16[2,128,4096]{2,1,0:T(8,128)(2,1)}), bf16[2,256,4096]{2,1,0:T(8,128)(2,1)}) %all-gather.6.cloned.1.call-update) | async-done | bytes 4194320 | tf_op jit(solution)/shard_map/all_gather | solution.py:133
  630.1 62.1 %while.18 = (s32[]{:T(128)}, f32[512,2,1,4096]{3,0,1,2:T(8,128)}, f32[512,2,1,4096]{3,0,1,2:T(8,128)}, bf16[2,256,4096]{2,1,0:T(8,128)(2,1)}, s32[]{:T(128)}, /*...) while((s32[]{:T(128)}, f32[512,2,1,4096]{3,0,1,2:T(8,128)}, ...), condition=%wide.region_66.67_spmd.clone, body=%wide.region_65.66_spmd.clone.sunk | while | flops 2197815296 | bytes 105390264 | solution.py:156
  642.5 14.2 %convert_add_fusion.12 = (f32[512,2,1,4096]{3,0,1,2:T(8,128)}, f32[512,2,1,4096]{3,0,1,2:T(8,128)}) fusion(f32[512,2,1,4096]{3,0,1,2:T(8,128)} %get-tuple-element.770, bf16[512,1,4096]{2,0,1:T(8,128)(2,1)S(1)} %bitcast.333, bf16[512,1,4096]{2,0,1:T(8,128)(2,1)S(1)} %bitcast.331, pred[]{:T(512)S(6)} %compare.57, bf16[512,1,4096]{2,0,1:T(8,128)(2,1)} %bitcast.334, ...), kind=kLoop, calls=%fused_computation.88.clone.1 | loop fusion | flops 33554432 | bytes 83886080 | tf_op jit(solution)/shard_map/while/body/eval_jaxpr/add | solution.py:153
  669.1 23.1 %convert_add_fusion.12 = (f32[512,2,1,4096]{3,0,1,2:T(8,128)}, f32[512,2,1,4096]{3,0,1,2:T(8,128)}) fusion(f32[512,2,1,4096]{3,0,1,2:T(8,128)} %get-tuple-element.770, bf16[512,1,4096]{2,0,1:T(8,128)(2,1)S(1)} %bitcast.333, bf16[512,1,4096]{2,0,1:T(8,128)(2,1)S(1)} %bitcast.331, pred[]{:T(512)S(6)} %compare.57, bf16[512,1,4096]{2,0,1:T(8,128)(2,1)} %bitcast.334, ...), kind=kLoop, calls=%fused_computation.88.clone.1 | loop fusion | flops 33554432 | bytes 83886080 | tf_op jit(solution)/shard_map/while/body/eval_jaxpr/add | solution.py:153
  692.2 28.6 %copy.38 = bf16[512,2,1,4096]{3,1,2,0:T(2,128)(2,1)} copy(f32[512,2,1,4096]{3,0,1,2:T(8,128)} %get-tuple-element.635) | data formatting | bytes 25165824 | tf_op jit(solution)/shard_map/while | solution.py:156
  720.7 18.6 %copy.39 = bf16[512,2,1,4096]{3,1,2,0:T(2,128)(2,1)} copy(f32[512,2,1,4096]{3,0,1,2:T(8,128)S(1)} %copy-done) | data formatting | bytes 25165824 | tf_op jit(solution)/shard_map/while | solution.py:156
  (221 shorter events, 217.9 us)
Async XLA Ops:
  8.0 27.0 %copy-start.3 = (bf16[2,16,4096]{2,1,0:T(8,128)(2,1)S(1)}, bf16[2,16,4096]{2,1,0:T(8,128)(2,1)}, u32[]{:S(2)}) copy-start(bf16[2,16,4096]{2,1,0:T(8,128)(2,1)} %param.38) | copy-start | bytes 786436
  27.0 7.9 %all-to-all-start = ((bf16[4,16,1024]{2,1,0:T(8,128)(2,1)}), bf16[4,16,1024]{2,1,0:T(8,128)(2,1)S(1)}, u32[]{:S(2)}, u32[]{:S(2)}) async-start(bf16[4,16,1024]{2,1,0:T(8,128)(2,1)} %bitcast.29), calls=%async_computation | async-start | bytes 262144 | tf_op jit(solution)/shard_map/all_to_all | solution.py:71
  35.0 6.8 collective-permute-start
  61.3 6.8 collective-permute-start.1
  82.4 6.8 collective-permute-start.2
  96.5 31.5 %copy-start.4 = (bf16[2,16,4096]{2,1,0:T(8,128)(2,1)S(1)}, bf16[2,16,4096]{2,1,0:T(8,128)(2,1)}, u32[]{:S(2)}) copy-start(bf16[2,16,4096]{2,1,0:T(8,128)(2,1)} %param.41) | copy-start | bytes 786436
  103.7 7.9 %collective-permute-start.3 = (bf16[16,4096]{1,0:T(8,128)(2,1)S(1)}, bf16[16,4096]{1,0:T(8,128)(2,1)S(1)}, u32[]{:S(2)}, u32[]{:S(2)}) collective-permute-start(bf16[16,4096]{1,0:T(8,128)(2,1)S(1)} %fusion.138), channel_id=1, source_target_pairs={{0,8},{8,16},{16,24},{24,0},{1,9},{9,17},{17,25},{25,1},{2,10},{10... | collective-permute-start | bytes 393224 | tf_op jit(solution)/shard_map/ppermute | solution.py:11
  124.6 7.9 %all-to-all-start.4 = ((bf16[4,16,1024]{2,1,0:T(8,128)(2,1)}), bf16[4,16,1024]{2,1,0:T(8,128)(2,1)S(1)}, u32[]{:S(2)}, u32[]{:S(2)}) async-start(bf16[4,16,1024]{2,1,0:T(8,128)(2,1)} %bitcast.45), calls=%async_computation.4 | async-start | bytes 262144 | tf_op jit(solution)/shard_map/all_to_all | solution.py:71
  127.9 88.2 %reduce-scatter.9.cloned.1.call-start = ((), (), s32[]{:S(2)}) async-start(), calls=%async_computation.17 | async-start | bytes 655360 | tf_op jit(solution)/shard_map/reduce_scatter | solution.py:107
  132.6 8.4 %collective-permute-start.4 = (bf16[16,4096]{1,0:T(8,128)(2,1)S(1)}, bf16[16,4096]{1,0:T(8,128)(2,1)S(1)}, u32[]{:S(2)}, u32[]{:S(2)}) collective-permute-start(bf16[16,4096]{1,0:T(8,128)(2,1)S(1)} %fusion.142), channel_id=1, source_target_pairs={{0,8},{8,16},{16,24},{24,0},{1,9},{9,17},{17,25},{25,1},{2,10},{10... | collective-permute-start | bytes 393224 | tf_op jit(solution)/shard_map/ppermute | solution.py:11
  139.8 0.8 copy-start.1
  154.8 7.9 %all-to-all-start.5 = ((bf16[4,16,1024]{2,1,0:T(8,128)(2,1)}), bf16[4,16,1024]{2,1,0:T(8,128)(2,1)S(1)}, u32[]{:S(2)}, u32[]{:S(2)}) async-start(bf16[4,16,1024]{2,1,0:T(8,128)(2,1)} %bitcast.49), calls=%async_computation.5 | async-start | bytes 262144 | tf_op jit(solution)/shard_map/all_to_all | solution.py:71
  162.8 7.9 %collective-permute-start.5 = (bf16[16,4096]{1,0:T(8,128)(2,1)S(1)}, bf16[16,4096]{1,0:T(8,128)(2,1)S(1)}, u32[]{:S(2)}, u32[]{:S(2)}) collective-permute-start(bf16[16,4096]{1,0:T(8,128)(2,1)S(1)} %fusion.146), channel_id=1, source_target_pairs={{0,8},{8,16},{16,24},{24,0},{1,9},{9,17},{17,25},{25,1},{2,10},{10... | collective-permute-start | bytes 393224 | tf_op jit(solution)/shard_map/ppermute | solution.py:11
  178.6 7.9 %all-to-all-start.6 = ((bf16[4,16,1024]{2,1,0:T(8,128)(2,1)}), bf16[4,16,1024]{2,1,0:T(8,128)(2,1)S(1)}, u32[]{:S(2)}, u32[]{:S(2)}) async-start(bf16[4,16,1024]{2,1,0:T(8,128)(2,1)} %bitcast.53), calls=%async_computation.6 | async-start | bytes 262144 | tf_op jit(solution)/shard_map/all_to_all | solution.py:71
  186.6 6.8 collective-permute-start.6
  201.3 7.9 %all-to-all-start.7 = ((bf16[4,16,1024]{2,1,0:T(8,128)(2,1)}), bf16[4,16,1024]{2,1,0:T(8,128)(2,1)S(1)}, u32[]{:S(2)}, u32[]{:S(2)}) async-start(bf16[4,16,1024]{2,1,0:T(8,128)(2,1)} %bitcast.57), calls=%async_computation.7 | async-start | bytes 262144 | tf_op jit(solution)/shard_map/all_to_all | solution.py:71
  204.7 60.7 %reduce-scatter.11.cloned.1.call-start = ((), (), s32[]{:S(2)}) async-start(), calls=%async_computation.18 | async-start | bytes 655360 | tf_op jit(solution)/shard_map/reduce_scatter | solution.py:107
  209.3 6.8 collective-permute-start.7
  219.2 8.8 %collective-permute-start.8 = (bf16[16,4096]{1,0:T(8,128)(2,1)S(1)}, bf16[16,4096]{1,0:T(8,128)(2,1)S(1)}, u32[]{:S(2)}, u32[]{:S(2)}) collective-permute-start(bf16[16,4096]{1,0:T(8,128)(2,1)S(1)} %fusion.162), channel_id=1, source_target_pairs={{0,24},{8,0},{16,8},{24,16},{1,25},{9,1},{17,9},{25,17},{2,26},{10... | collective-permute-start | bytes 393224 | tf_op jit(solution)/shard_map/ppermute | solution.py:11
  235.0 0.8 copy-start.2
  235.9 73.4 %reduce-scatter.13.cloned.1.call-start = ((), (), s32[]{:S(2)}) async-start(), calls=%async_computation.19 | async-start | bytes 655360 | tf_op jit(solution)/shard_map/reduce_scatter | solution.py:107
  268.1 6.3 collective-permute-start.9
  282.6 68.5 %reduce-scatter.15.cloned.1.call-start = ((), (), s32[]{:S(2)}) async-start(), calls=%async_computation.20 | async-start | bytes 655360 | tf_op jit(solution)/shard_map/reduce_scatter | solution.py:107
  311.4 6.0 collective-permute-start.10
  331.2 65.1 %reduce-scatter.17.cloned.1.call-start = ((), (), s32[]{:S(2)}) async-start(), calls=%async_computation.21 | async-start | bytes 655360 | tf_op jit(solution)/shard_map/reduce_scatter | solution.py:107
  353.1 6.0 collective-permute-start.11
  373.0 68.7 %reduce-scatter.19.cloned.1.call-start = ((), (), s32[]{:S(2)}) async-start(), calls=%async_computation.22 | async-start | bytes 655360 | tf_op jit(solution)/shard_map/reduce_scatter | solution.py:107
  398.5 6.0 collective-permute-start.12
  412.3 73.0 %reduce-scatter.21.cloned.1.call-start = ((), (), s32[]{:S(2)}) async-start(), calls=%async_computation.23 | async-start | bytes 655360 | tf_op jit(solution)/shard_map/reduce_scatter | solution.py:107
  443.9 6.0 collective-permute-start.13
  449.9 0.6 copy-start.5
  458.5 71.8 %reduce-scatter.23.cloned.1.call-start = ((), (), s32[]{:S(2)}) async-start(), calls=%async_computation.24 | async-start | bytes 655360 | tf_op jit(solution)/shard_map/reduce_scatter | solution.py:107
  487.5 10.3 %collective-permute-start.14 = (bf16[16,4096]{1,0:T(8,128)(2,1)S(1)}, bf16[16,4096]{1,0:T(8,128)(2,1)S(1)}, u32[]{:S(2)}, u32[]{:S(2)}) collective-permute-start(bf16[16,4096]{1,0:T(8,128)(2,1)S(1)} %fusion.192), channel_id=1, source_target_pairs={{0,24},{8,0},{16,8},{24,16},{1,25},{9,1},{17,9},{25,17},{2,26},{10... | collective-permute-start | bytes 393224 | tf_op jit(solution)/shard_map/ppermute | solution.py:11
  506.4 65.1 %all-gather.4.cloned.1.call-start = ((), (), s32[]{:S(2)}) async-start(), calls=%async_computation.16 | async-start | bytes 6291456 | tf_op jit(solution)/shard_map/all_gather | solution.py:132
  512.7 117.4 %all-gather.6.cloned.1.call-start = ((), (), s32[]{:S(2)}) async-start(), calls=%async_computation.25 | async-start | bytes 6291456 | tf_op jit(solution)/shard_map/all_gather | solution.py:133
  532.4 6.0 collective-permute-start.15
  692.2 28.6 %copy-start = (f32[512,2,1,4096]{3,0,1,2:T(8,128)S(1)}, f32[512,2,1,4096]{3,0,1,2:T(8,128)}, u32[]{:S(2)}) copy-start(f32[512,2,1,4096]{3,0,1,2:T(8,128)} %get-tuple-element.634) | copy-start | bytes 50331652
Sparse Core Ops, SparseCore 0:
  140.8 28.8 reduce-scatter.8
  236.0 29.3 reduce-scatter.10
  282.7 26.5 reduce-scatter.12
  331.4 19.5 reduce-scatter.14
  373.1 23.2 reduce-scatter.16
  412.4 29.3 reduce-scatter.18
  458.6 26.6 reduce-scatter.20
  506.5 23.7 reduce-scatter.22
Sparse Core Ops, SparseCore 1:
  512.7 58.7 all-gather.3
  573.5 56.6 all-gather.5
where the time goes:
time: 757 us; the launch traced here: 747 us
  waiting for transfers between devices  306 us (40%)
  blocking collectives  149 us (20%)
  local copies, waits for them, and re-layouts  87.8 us (12%)
  other arithmetic  68.5 us (9%)
  matrix products  61 us (8%)
  starting transfers between devices  56.4 us (7%)
  between operations  17.6 us (2%)
    reduce_scatter x8, waiting for transfers between devices, body(): lax.psum_scatter(partial_rows(jnp.int32(0), shard_rows * lax.axis_size('t...  151 us
    all_gather x9, blocking collectives, body(): gathered = lax.all_gather(normed, 'tensor', axis=0, tiled=True)  65 us
    all_gather x9, blocking collectives, body(): gathered = lax.all_gather(current, 'tensor', axis=0, tiled=True)  63.2 us
    all_gather x1, waiting for transfers between devices, body(): lax.all_gather(grad_tokens, 'dp', axis=1, tiled=True)  58.6 us
    ppermute x16, waiting for transfers between devices, passed_along(): lax.ppermute(array, axis, [(i, (i + by) % peers) for i in range(peers)])  49.2 us
    while x2, local copies, waits for them, and re-layouts, body(): lax.fori_loop(0, pieces[0].shape[1] // group_size, one_group, (empty, emp...  47.2 us
    ppermute x16, starting transfers between devices, passed_along(): lax.ppermute(array, axis, [(i, (i + by) % peers) for i in range(peers)])  39.4 us
    add x2, other arithmetic, one_group(): updated.append(totals[factor_pick] + jnp.stack(partials, 1)[:, :, None, :])  37.3 us
  transfers between devices with their start and end apart: 31, of which 28 were waited for; matrix products, arithmetic and copies ran while one was open for 7% of the time, Pallas kernels for 0%

commit v1 on v0

v1 whole, which is shorter than its diff:
```python
import functools

import jax
import jax.numpy as jnp
from jax import lax
from jax.experimental import pallas as pl
from jax.experimental.pallas import tpu as pltpu
from jax.sharding import PartitionSpec as P

EPSILON = 1e-05


def peer_of(c, k):
    return lax.rem(c // 2 + k // 2, 2) * 2 + lax.rem(c + k, 2)


def chain_kernel(
    dims,
    x_ref,
    w_hbm,
    g_ref,
    cot_ref,
    h_out,
    d_out,
    w,
    hbuf,
    dbuf,
    acc,
    nxt,
    psend,
    rbuf,
    dnext,
    w_sem,
    own_sem,
    in_send,
    in_recv,
    f1_send,
    f1_recv,
    fx_send,
    fx_recv,
    b1_send,
    b1_recv,
    bx_send,
    bx_recv,
    rs_send,
    rs_recv,
    dp_send,
    dp_recv,
    loc_sem,
):
    micro, slots, rows, width, quarter, pipes, tensors, dps = dims
    items = slots * micro
    layers = slots * pipes
    group = tensors * rows
    p = lax.axis_index("pipe")
    c = lax.axis_index("tensor")
    d = lax.axis_index("dp")
    after = lax.rem(p + 1, pipes)
    before = lax.rem(p + pipes - 1, pipes)

    def where(pp, cc, dd):
        return {"pipe": pp, "tensor": cc, "dp": dd}

    def remote(src, dst, send, recv, target):
        return pltpu.make_async_remote_copy(
            src_ref=src,
            dst_ref=dst,
            send_sem=send,
            recv_sem=recv,
            device_id=target,
            device_id_type=pl.DeviceIdType.MESH,
        )

    w_copies = [
        pltpu.make_async_copy(w_hbm.at[s, 0], w.at[s], w_sem.at[s]) for s in range(slots)
    ]
    for copy in w_copies:
        copy.start()

    barrier = pltpu.get_barrier_semaphore()
    partners = [where(p, peer_of(c, k), d) for k in range(1, tensors)]
    partners += [where(after, c, d), where(before, c, d)]
    partners += [where(p, c, lax.rem(d + k, dps)) for k in range(1, dps)]
    for partner in partners:
        pl.semaphore_signal(
            barrier, inc=1, device_id=partner, device_id_type=pl.DeviceIdType.MESH
        )
    pl.semaphore_wait(barrier, len(partners))

    def row_ds(cc):
        return pl.ds(pl.multiple_of(cc * rows, rows), rows)

    def col_ds(cc):
        return pl.ds(pl.multiple_of(cc * quarter, quarter), quarter)

    def opening(src, buf, m, k):
        return remote(
            src.at[m],
            buf.at[m, row_ds(c)],
            in_send.at[m, k - 1],
            in_recv.at[m, k - 1],
            where(p, peer_of(c, k), d),
        )

    def opening_all(src, buf):
        for m in range(micro):
            for k in range(1, tensors):
                opening(src, buf, m, k).start()
        for m in range(micro):
            pltpu.make_async_copy(src.at[m], buf.at[m, row_ds(c)], own_sem.at[m]).start()

    def opening_wait(src, buf, m):
        pltpu.make_async_copy(src.at[m], buf.at[m, row_ds(c)], own_sem.at[m]).wait()
        for k in range(1, tensors):
            opening(src, buf, m, k).wait_recv()

    @pl.when(p == 0)
    def _():
        opening_all(x_ref, hbuf)

    @pl.when(p == pipes - 1)
    def _():
        opening_all(cot_ref, dbuf)

    def to_dp(buf, out, item, slot, m, which, k):
        return remote(
            buf.at[item],
            out.at[slot, d, m],
            dp_send.at[which, item, k - 1],
            dp_recv.at[which, item, k - 1],
            where(p, c, lax.rem(d + k, dps)),
        )

    def to_own(buf, out, item, slot, m, which):
        return pltpu.make_async_copy(
            buf.at[item], out.at[slot, d, m], loc_sem.at[which, item]
        )

    def f_slice(item, cc):
        return hbuf.at[item, :, col_ds(cc)]

    def f_along(item, target_item):
        return remote(
            nxt.at[item],
            f_slice(target_item, c),
            f1_send.at[item],
            f1_recv.at[target_item],
            where(after, c, d),
        )

    def spread(make_slice, item, part, send, recv):
        owner = peer_of(c, 2) if part == 2 else c
        target = peer_of(c, 2) if part == 1 else peer_of(c, 1)
        ref = make_slice(item, owner)
        return remote(ref, ref, send.at[item, part], recv.at[item, part], where(p, target, d))

    def f_step(item, carry):
        slot = item // micro
        m = lax.rem(item, micro)
        layer = slot * pipes + p
        target_item = item + micro * ((p + 1) // pipes)

        @pl.when(m == 0)
        def _():
            pltpu.make_async_copy(w_hbm.at[slot, 0], w.at[slot], w_sem.at[slot]).wait()

        fx = functools.partial(spread, f_slice, item, send=fx_send, recv=fx_recv)

        @pl.when(layer == 0)
        def _():
            opening_wait(x_ref, hbuf, item)

        @pl.when(layer > 0)
        def _():
            f_along(item, item).wait_recv()
            fx(part=1).start()
            fx(part=0).start()

        def piece(cc, first):
            part = hbuf[item, :, col_ds(cc)].astype(jnp.float32)
            scaled = (part * g_ref[slot, :, col_ds(cc)]).astype(jnp.bfloat16)
            product = jnp.dot(scaled, w[slot, col_ds(cc), :], preferred_element_type=jnp.float32)
            if first:
                acc[...] = product
            else:
                acc[...] += product
            return jnp.sum(part * part, axis=-1, keepdims=True)

        total = piece(c, True)

        @pl.when(layer > 0)
        def _():
            fx(part=0).wait_recv()

        total += piece(peer_of(c, 1), False)

        @pl.when(layer > 0)
        def _():
            fx(part=1).wait_recv()
            fx(part=2).start()

        total += piece(peer_of(c, 2), False)

        @pl.when(layer > 0)
        def _():
            fx(part=2).wait_recv()

        total += piece(peer_of(c, 3), False)

        @pl.when(layer < layers - 1)
        def _():
            inverse_rms = lax.rsqrt(total * (1.0 / width) + EPSILON)
            product = (acc[...] * inverse_rms).astype(jnp.bfloat16).astype(jnp.float32)
            nxt[item] = (hbuf[item, :, col_ds(c)].astype(jnp.float32) + product).astype(
                jnp.bfloat16
            )
            f_along(item, target_item).start()

        to_own(hbuf, h_out, item, slot, m, 0).start()
        for k in range(1, dps):
            to_dp(hbuf, h_out, item, slot, m, 0, k).start()
        return carry

    lax.fori_loop(0, items, f_step, 0)

    def b_slice(item, cc):
        return dbuf.at[item, row_ds(cc)]

    def b_along(item, target_item):
        return remote(
            dnext.at[item],
            b_slice(target_item, c),
            b1_send.at[item],
            b1_recv.at[target_item],
            where(before, c, d),
        )

    blocks = width // quarter

    def reduce_copy(item, k, n):
        return remote(
            psend.at[item, row_ds(peer_of(c, k)), pl.ds(n * quarter, quarter)],
            rbuf.at[item, k - 1, :, pl.ds(n * quarter, quarter)],
            rs_send.at[item, k - 1, n],
            rs_recv.at[item, k - 1, n],
            where(p, peer_of(c, k), d),
        )

    def b_step(item, carry):
        slot = slots - 1 - item // micro
        m = lax.rem(item, micro)
        layer = slot * pipes + p
        target_item = item + micro * (1 - (p + pipes - 1) // pipes)
        bx = functools.partial(spread, b_slice, item, send=bx_send, recv=bx_recv)

        @pl.when(layer == layers - 1)
        def _():
            opening_wait(cot_ref, dbuf, item)

        @pl.when(layer < layers - 1)
        def _():
            b_along(item, item).wait_recv()
            bx(part=1).start()
            bx(part=0).start()
            bx(part=1).wait_recv()
            bx(part=2).start()
            bx(part=0).wait_recv()
            bx(part=2).wait_recv()

        @pl.when(layer > 0)
        def _():
            columns = dbuf[item, :, col_ds(c)]
            for n in range(blocks):
                psend[item, :, n * quarter : (n + 1) * quarter] = lax.dot_general(
                    columns,
                    w[slot, n * quarter : (n + 1) * quarter, :],
                    (((1,), (1,)), ((), ())),
                    preferred_element_type=jnp.float32,
                ).astype(jnp.bfloat16)
                for k in range(tensors - 1, 0, -1):
                    reduce_copy(item, k, n).start()

        to_own(dbuf, d_out, item, slot, m, 1).start()
        for k in range(1, dps):
            to_dp(dbuf, d_out, item, slot, m, 1, k).start()

        @pl.when(layer > 0)
        def _():
            for n in range(blocks):
                for k in range(1, tensors):
                    reduce_copy(item, k, n).wait_recv()
            own = row_ds(c)
            stored = slot * micro + m
            squares = jnp.zeros((rows, 1), jnp.float32)
            inner = jnp.zeros((rows, 1), jnp.float32)
            kept = []
            for n in range(blocks):
                cut = slice(n * quarter, (n + 1) * quarter)
                back = psend[item, own, cut].astype(jnp.float32)
                for k in range(1, tensors):
                    back += rbuf[item, k - 1, :, cut].astype(jnp.float32)
                scaled = g_ref[slot, :, cut] * back
                hidden = hbuf[stored, own, cut].astype(jnp.float32)
                squares += jnp.sum(hidden * hidden, axis=-1, keepdims=True)
                inner += jnp.sum(hidden * scaled, axis=-1, keepdims=True)
                kept.append(scaled)
            inverse_rms = lax.rsqrt(squares * (1.0 / width) + EPSILON)
            factor = inverse_rms * inverse_rms * inverse_rms * (inner * (1.0 / width))
            for n in range(blocks):
                cut = slice(n * quarter, (n + 1) * quarter)
                dnext[item, :, cut] = (
                    dbuf[item, own, cut].astype(jnp.float32)
                    + inverse_rms * kept[n]
                    - factor * hbuf[stored, own, cut].astype(jnp.float32)
                ).astype(jnp.bfloat16)
            b_along(item, target_item).start()

        return carry

    lax.fori_loop(0, items, b_step, 0)

    @pl.when(p == 0)
    def _():
        for m in range(micro):
            for k in range(1, tensors):
                opening(x_ref, hbuf, m, k).wait_send()

    @pl.when(p == pipes - 1)
    def _():
        for m in range(micro):
            for k in range(1, tensors):
                opening(cot_ref, dbuf, m, k).wait_send()

    def ending(item, carry):
        f_slot = item // micro
        b_slot = slots - 1 - item // micro
        m = lax.rem(item, micro)
        f_layer = f_slot * pipes + p
        b_layer = b_slot * pipes + p

        @pl.when(f_layer > 0)
        def _():
            for part in range(3):
                spread(f_slice, item, part, fx_send, fx_recv).wait_send()

        @pl.when(f_layer < layers - 1)
        def _():
            f_along(item, item).wait_send()

        @pl.when(b_layer < layers - 1)
        def _():
            for part in range(3):
                spread(b_slice, item, part, bx_send, bx_recv).wait_send()

        @pl.when(b_layer > 0)
        def _():
            b_along(item, item).wait_send()
            for n in range(blocks):
                for k in range(1, tensors):
                    reduce_copy(item, k, n).wait_send()

        to_own(hbuf, h_out, item, f_slot, m, 0).wait()
        to_own(dbuf, d_out, item, b_slot, m, 1).wait()
        for k in range(1, dps):
            to_dp(hbuf, h_out, item, f_slot, m, 0, k).wait()
            to_dp(dbuf, d_out, item, b_slot, m, 1, k).wait()
        return carry

    lax.fori_loop(0, items, ending, 0)


def chain(inputs, weights, norm_gains, cotangent):
    micro, rows, width = inputs.shape
    slots = weights.shape[0]
    quarter = weights.shape[3]
    pipes = lax.axis_size("pipe")
    tensors = lax.axis_size("tensor")
    dps = lax.axis_size("dp")
    items = slots * micro
    group = tensors * rows
    blocks = width // quarter
    dims = (micro, slots, rows, width, quarter, pipes, tensors, dps)
    vmem = pl.BlockSpec(memory_space=pltpu.VMEM)
    hbm = pl.BlockSpec(memory_space=pl.ANY)
    dma = pltpu.SemaphoreType.DMA
    out = jax.ShapeDtypeStruct((slots, dps, micro, group, width), jnp.bfloat16)
    return pl.pallas_call(
        functools.partial(chain_kernel, dims),
        out_shape=(out, out),
        in_specs=[vmem, hbm, vmem, vmem],
        out_specs=(hbm, hbm),
        scratch_shapes=[
            pltpu.VMEM((slots, width, quarter), jnp.bfloat16),
            pltpu.VMEM((items, group, width), jnp.bfloat16),
            pltpu.VMEM((items, group, width), jnp.bfloat16),
            pltpu.VMEM((group, quarter), jnp.float32),
            pltpu.VMEM((items, group, quarter), jnp.bfloat16),
            pltpu.VMEM((items, group, width), jnp.bfloat16),
            pltpu.VMEM((items, tensors - 1, rows, width), jnp.bfloat16),
            pltpu.VMEM((items, rows, width), jnp.bfloat16),
            dma((slots,)),
            dma((micro,)),
            dma((micro, tensors - 1)),
            dma((micro, tensors - 1)),
            dma((items,)),
            dma((items,)),
            dma((items, 3)),
            dma((items, 3)),
            dma((items,)),
            dma((items,)),
            dma((items, 3)),
            dma((items, 3)),
            dma((items, tensors - 1, blocks)),
            dma((items, tensors - 1, blocks)),
            dma((2, items, dps - 1)),
            dma((2, items, dps - 1)),
            dma((2, items)),
        ],
        compiler_params=pltpu.CompilerParams(
            collective_id=0, has_side_effects=True, vmem_limit_bytes=56 * 1024 * 1024
        ),
        name="chain",
    )(inputs, weights, norm_gains, cotangent)


def body(inputs, weights, norm_gains, cotangent):
    micro, rows, width = inputs.shape
    slots = weights.shape[0]
    quarter = weights.shape[3]
    tensors = lax.axis_size("tensor")
    dps = lax.axis_size("dp")
    own_rows = quarter // dps
    tokens = micro * rows * tensors * dps
    scale = 1.0 / tokens
    h_all, d_all = chain(inputs, weights, norm_gains, cotangent)
    base = (lax.axis_index("tensor") * dps + lax.axis_index("dp")) * own_rows
    h_all = h_all.reshape(slots, tokens, width)
    d_all = d_all.reshape(slots, tokens, width)
    wide = h_all.astype(jnp.float32)
    inverse_rms = lax.rsqrt(jnp.mean(wide * wide, axis=-1, keepdims=True) + EPSILON)
    normed = (wide * inverse_rms * norm_gains).astype(jnp.bfloat16)

    def factor(block):
        parts = []
        for s in range(slots):
            columns = lax.dynamic_slice_in_dim(block[s], base, own_rows, 1)
            gram = lax.dot_general(
                columns, block[s], (((0,), (0,)), ((), ())), preferred_element_type=jnp.float32
            )
            parts.append((gram * scale).astype(jnp.bfloat16))
        return jnp.stack(parts, 1)[:, :, None, :]

    return factor(normed), factor(d_all)


def solution(mesh):
    in_specs = (
        P(None, ("tensor", "dp"), None),
        P(None, "pipe", None, "tensor"),
        P(None, "pipe", None),
        P(None, ("tensor", "dp"), None),
    )
    out_specs = (P(("tensor", "dp"), None, "pipe", None), P(("tensor", "dp"), None, "pipe", None))
    return jax.shard_map(body, mesh=mesh, in_specs=in_specs, out_specs=out_specs, check_vma=False)
```

time: 757 us -> 332 us (0.44); the launches traced: 747 us -> 332 us
  waiting for transfers between devices: 306 us -> 0 us
  Pallas kernels: 0 us -> 262 us
  blocking collectives: 149 us -> 0 us
  starting transfers between devices: 56.4 us -> 0 us
  matrix products: 61 us -> 11.1 us
  other arithmetic: 68.5 us -> 18.6 us
  local copies, waits for them, and re-layouts: 87.8 us -> 39.8 us
  between operations: 17.6 us -> 0.68 us
    pallas_call x0 -> x1, Pallas kernels: none -> 262 us  [chain(): pl.pallas_call(functools.partial(chain_kernel, dims), out_shape=(out, out...]
    reduce_scatter x8 -> x0, waiting for transfers between devices: 151 us -> none  [body(): lax.psum_scatter(partial_rows(jnp.int32(0), shard_rows * lax.axis_size('t...]
    all_gather x18 -> x0, blocking collectives: 128 us -> none  [the longest x9 65 us: body(): gathered = lax.all_gather(normed, 'tensor', axis=0, tiled=True)]
    all_gather x2 -> x0, waiting for transfers between devices: 83.6 us -> none  [the longest x1 58.6 us: body(): lax.all_gather(grad_tokens, 'dp', axis=1, tiled=True)]
    dot_general x14 -> x4, matrix products: 61 us -> 11.1 us  [factor(): lax.dot_general(columns, block[s], (((0,), (0,)), ((), ())), preferred_el...]
    ppermute x16 -> x0, waiting for transfers between devices: 49.2 us -> none  [passed_along(): lax.ppermute(array, axis, [(i, (i + by) % peers) for i in range(peers)])]
    while x2 -> x0, local copies, waits for them, and re-layouts: 47.2 us -> none  [body(): lax.fori_loop(0, pieces[0].shape[1] // group_size, one_group, (empty, emp...]
    ppermute x16 -> x0, starting transfers between devices: 39.4 us -> none  [passed_along(): lax.ppermute(array, axis, [(i, (i + by) % peers) for i in range(peers)])]
  transfers between devices with their start and end apart: 31 -> 0, of which waited for: 28 -> 0; matrix products, arithmetic and copies ran while one was open for 7% -> 0% of each run, Pallas kernels for 0% -> 0%
where the time goes in v1:
time: 332 us
  Pallas kernels  262 us (79%)
  local copies, waits for them, and re-layouts  39.8 us (12%)
  other arithmetic  18.6 us (6%)
  matrix products  11.1 us (3%)
    pallas_call x1, Pallas kernels, chain(): pl.pallas_call(functools.partial(chain_kernel, dims), out_shape=(out, out...  262 us
    unnamed x9, local copies, waits for them, and re-layouts  34 us
    broadcast_in_dim x2, other arithmetic, factor(): return jnp.stack(parts, 1)[:, :, None, :]  13.8 us
    dot_general x4, matrix products, factor(): lax.dot_general(columns, block[s], (((0,), (0,)), ((), ())), preferred_el...  11.1 us

profile of v1, /device:TPU:0, one launch (start us, length us, event | category | flops | bytes accessed | tf_op | source)
XLA Modules:
  0.0 332.0 jit_solution(16249989564967426037)
XLA Ops:
  0.6 0.8 copy.10
  1.4 261.8 %chain.1 = (bf16[2,2,2,64,4096]{4,3,2,1,0:T(8,128)(2,1)}, bf16[2,2,2,64,4096]{4,3,2,1,0:T(8,128)(2,1)}) custom-call(bf16[2,16,4096]{2,1,0:T(8,128)(2,1)} %x_ref.1, bf16[2,1,4096,1024]{3,2,1,0:T(8,128)(2,1)} %w_hbm.1, f32[2,1,4096]{2,1,0:T(1,128)} %g_ref.1, bf16[2,16,4096]{2,1,0:T(8,128)(2,1)} %cot_ref.1), custom_call_target="tpu_custom_call" | custom-call | tf_op jit(solution)/shard_map/chain/pallas_call | solution.py:387
  263.2 0.0 copy-start
  263.2 4.1 %fusion.18 = (bf16[1,2,2,64,4096]{4,3,2,1,0:T(8,128)(2,1)S(1)}, bf16[1,2,2,64,4096]{4,3,2,1,0:T(8,128)(2,1)}) fusion(bf16[2,2,2,64,4096]{4,3,2,1,0:T(8,128)(2,1)} %get-tuple-element.5), kind=kLoop, calls=%fused_computation.28 | loop fusion | bytes 8388608 | tf_op jit(solution)/shard_map/slice | solution.py:446
  267.3 0.0 copy-done
  267.3 0.9 multiply_reduce_fusion
  268.2 0.1 rsqrt.12
  268.3 3.8 %fusion.1 = bf16[2,256,4096]{2,1,0:T(8,128)(2,1)S(1)} fusion(f32[2,4096]{1,0:T(2,128)S(1)} %bitcast.39, f32[2,256]{1,0:T(2,128)S(1)} %rsqrt.12, bf16[2,2,2,64,4096]{4,3,2,1,0:T(8,128)(2,1)} %get-tuple-element.4), kind=kLoop, calls=%fused_computation.4 | loop fusion | flops 8388608 | bytes 8423424 | tf_op jit(solution)/shard_map/convert_element_type | solution.py:441
  272.1 1.7 fusion.19
  273.8 0.0 copy-start.1
  273.8 1.3 fusion.2
  275.1 0.3 copy-done.1
  275.4 3.3 fusion.5
  278.7 3.2 fusion.4
  281.9 7.6 %maximum_bitcast_fusion.1 = bf16[512,2,1,4096]{3,0,1,2:T(8,128)(2,1)} fusion(bf16[512,1,4096]{2,0,1:T(8,128)(2,1)} %fusion.5, bf16[512,1,4096]{2,0,1:T(8,128)(2,1)} %fusion.4), kind=kLoop, calls=%fused_computation.1 | loop fusion | flops 4194304 | bytes 16777216 | tf_op jit(solution)/shard_map/broadcast_in_dim | solution.py:451
  289.6 0.0 copy-start.2
  289.6 16.5 %copy.7 = bf16[512,2,1,4096]{3,1,2,0:T(2,128)(2,1)} copy(bf16[512,2,1,4096]{3,0,1,2:T(8,128)(2,1)} %maximum_bitcast_fusion.1) | data formatting | bytes 16777216
  306.1 0.0 copy-done.2
  306.1 3.3 fusion.3
  309.4 6.2 %maximum_bitcast_fusion = bf16[512,2,1,4096]{3,0,1,2:T(8,128)(2,1)} fusion(bf16[512,1,4096]{2,0,1:T(8,128)(2,1)} %fusion.3, bf16[512,1,4096]{2,0,1:T(8,128)(2,1)S(1)} %fusion.2), kind=kLoop, calls=%fused_computation | loop fusion | flops 4194304 | bytes 16777216 | tf_op jit(solution)/shard_map/broadcast_in_dim | solution.py:451
  315.6 16.4 %copy.6 = bf16[512,2,1,4096]{3,1,2,0:T(2,128)(2,1)} copy(bf16[512,2,1,4096]{3,0,1,2:T(8,128)(2,1)} %maximum_bitcast_fusion) | data formatting | bytes 16777216
  (1 shorter events, 0.0 us)
Async XLA Ops:
  263.2 4.1 %copy-start = (bf16[2,2,2,64,4096]{4,3,2,1,0:T(8,128)(2,1)S(1)}, bf16[2,2,2,64,4096]{4,3,2,1,0:T(8,128)(2,1)}, u32[]{:S(2)}) copy-start(bf16[2,2,2,64,4096]{4,3,2,1,0:T(8,128)(2,1)} %get-tuple-element.4) | copy-start | bytes 12582916
  273.8 1.6 copy-start.1
  289.6 16.5 %copy-start.2 = (bf16[1,256,4096]{2,1,0:T(8,128)(2,1)S(1)}, bf16[1,256,4096]{2,1,0:T(8,128)(2,1)}, u32[]{:S(2)}) copy-start(bf16[1,256,4096]{2,1,0:T(8,128)(2,1)} %get-tuple-element.11) | copy-start | bytes 6291460

commit v2 on v1

v2 whole, which is shorter than its diff:
```python
import functools

import jax
import jax.numpy as jnp
from jax import lax
from jax.experimental import pallas as pl
from jax.experimental.pallas import tpu as pltpu
from jax.sharding import PartitionSpec as P

EPSILON = 1e-05


def peer_of(c, k):
    return lax.rem(c // 2 + k // 2, 2) * 2 + lax.rem(c + k, 2)


def chain_kernel(
    dims,
    x_ref,
    w_hbm,
    g_ref,
    cot_ref,
    h_out,
    d_out,
    w,
    hbuf,
    dcol,
    rms,
    acc,
    nxt,
    psend,
    rbuf,
    dnext,
    isend,
    irecv,
    w_sem,
    own_sem,
    in_send,
    in_recv,
    f1_send,
    f1_recv,
    fx_send,
    fx_recv,
    b1_send,
    b1_recv,
    rs_send,
    rs_recv,
    is_send,
    is_recv,
    dp_send,
    dp_recv,
    dg_send,
    dg_recv,
    loc_sem,
):
    micro, slots, rows, width, quarter, pipes, tensors, dps, cuts = dims
    items = slots * micro
    layers = slots * pipes
    group = tensors * rows
    part_rows = group // cuts
    p = lax.axis_index("pipe")
    c = lax.axis_index("tensor")
    d = lax.axis_index("dp")
    after = lax.rem(p + 1, pipes)
    before = lax.rem(p + pipes - 1, pipes)

    def where(pp, cc, dd):
        return {"pipe": pp, "tensor": cc, "dp": dd}

    def remote(src, dst, send, recv, target):
        return pltpu.make_async_remote_copy(
            src_ref=src,
            dst_ref=dst,
            send_sem=send,
            recv_sem=recv,
            device_id=target,
            device_id_type=pl.DeviceIdType.MESH,
        )

    w_copies = [
        pltpu.make_async_copy(w_hbm.at[s, 0], w.at[s], w_sem.at[s]) for s in range(slots)
    ]
    for copy in w_copies:
        copy.start()

    barrier = pltpu.get_barrier_semaphore()
    partners = [where(p, peer_of(c, k), d) for k in range(1, tensors)]
    partners += [where(after, c, d), where(before, c, d)]
    partners += [
        where(p, peer_of(c, k), lax.rem(d + e, dps)) for e in range(1, dps) for k in range(tensors)
    ]
    for partner in partners:
        pl.semaphore_signal(
            barrier, inc=1, device_id=partner, device_id_type=pl.DeviceIdType.MESH
        )
    pl.semaphore_wait(barrier, len(partners))

    def row_ds(cc):
        return pl.ds(pl.multiple_of(cc * rows, rows), rows)

    def col_ds(cc):
        return pl.ds(pl.multiple_of(cc * quarter, quarter), quarter)

    def opening(src, buf, m, k):
        whole = buf is hbuf
        return remote(
            src.at[m] if whole else src.at[m, :, col_ds(peer_of(c, k))],
            buf.at[m, row_ds(c)],
            in_send.at[m, k - 1],
            in_recv.at[m, k - 1],
            where(p, peer_of(c, k), d),
        )

    def opening_own(src, buf, m):
        whole = buf is hbuf
        return pltpu.make_async_copy(
            src.at[m] if whole else src.at[m, :, col_ds(c)], buf.at[m, row_ds(c)], own_sem.at[m]
        )

    def opening_all(src, buf):
        for m in range(micro):
            for k in range(1, tensors):
                opening(src, buf, m, k).start()
        for m in range(micro):
            opening_own(src, buf, m).start()

    def opening_wait(src, buf, m):
        opening_own(src, buf, m).wait()
        for k in range(1, tensors):
            opening(src, buf, m, k).wait_recv()

    @pl.when(p == 0)
    def _():
        opening_all(x_ref, hbuf)

    @pl.when(p == pipes - 1)
    def _():
        opening_all(cot_ref, dcol)

    def to_dp(item, slot, m, k):
        return remote(
            hbuf.at[item],
            h_out.at[slot, d, m],
            dp_send.at[item, k - 1],
            dp_recv.at[item, k - 1],
            where(p, c, lax.rem(d + k, dps)),
        )

    def to_own(item, slot, m):
        return pltpu.make_async_copy(hbuf.at[item], h_out.at[slot, d, m], loc_sem.at[0, item])

    def d_own(item, slot, m):
        return pltpu.make_async_copy(
            dcol.at[item], d_out.at[slot, d, m, :, col_ds(c)], loc_sem.at[1, item]
        )

    def d_share(item, slot, m, e, k):
        return remote(
            dcol.at[item],
            d_out.at[slot, d, m, :, col_ds(c)],
            dg_send.at[item, e, k],
            dg_recv.at[item, e, k],
            where(p, peer_of(c, k), lax.rem(d + e, dps)),
        )

    def d_shares(item, slot, m):
        return [
            d_share(item, slot, m, e, k)
            for e in range(dps - 1, -1, -1)
            for k in range(tensors - 1, -1, -1)
            if e or k
        ]

    def f_slice(item, cc, r):
        return hbuf.at[item, r * part_rows : (r + 1) * part_rows, col_ds(cc)]

    def f_along(item, target_item, r):
        return remote(
            nxt.at[item, r * part_rows : (r + 1) * part_rows],
            f_slice(target_item, c, r),
            f1_send.at[item, r],
            f1_recv.at[target_item, r],
            where(after, c, d),
        )

    def spread(item, part, r):
        owner = peer_of(c, 2) if part == 2 else c
        target = peer_of(c, 2) if part == 1 else peer_of(c, 1)
        ref = f_slice(item, owner, r)
        return remote(
            ref, ref, fx_send.at[item, part, r], fx_recv.at[item, part, r], where(p, target, d)
        )

    def f_step(item, carry):
        slot = item // micro
        m = lax.rem(item, micro)
        layer = slot * pipes + p
        target_item = item + micro * ((p + 1) // pipes)

        @pl.when(m == 0)
        def _():
            pltpu.make_async_copy(w_hbm.at[slot, 0], w.at[slot], w_sem.at[slot]).wait()

        @pl.when(layer == 0)
        def _():
            opening_wait(x_ref, hbuf, item)

        @pl.when(layer > 0)
        def _():
            for r in range(cuts):
                f_along(item, item, r).wait_recv()
                spread(item, 1, r).start()
                spread(item, 0, r).start()

        def piece(cc, first):
            part = hbuf[item, :, col_ds(cc)].astype(jnp.float32)
            scaled = (part * g_ref[slot, :, col_ds(cc)]).astype(jnp.bfloat16)
            product = jnp.dot(scaled, w[slot, col_ds(cc), :], preferred_element_type=jnp.float32)
            if first:
                acc[...] = product
            else:
                acc[...] += product
            return jnp.sum(part * part, axis=-1, keepdims=True)

        total = piece(c, True)

        @pl.when(layer > 0)
        def _():
            for r in range(cuts):
                spread(item, 0, r).wait_recv()

        total += piece(peer_of(c, 1), False)

        @pl.when(layer > 0)
        def _():
            for r in range(cuts):
                spread(item, 1, r).wait_recv()
                spread(item, 2, r).start()

        total += piece(peer_of(c, 2), False)

        @pl.when(layer > 0)
        def _():
            for r in range(cuts):
                spread(item, 2, r).wait_recv()

        total += piece(peer_of(c, 3), False)

        inverse_rms = lax.rsqrt(total * (1.0 / width) + EPSILON)
        rms[item] = jnp.broadcast_to(inverse_rms, (group, 128))

        @pl.when(layer < layers - 1)
        def _():
            product = (acc[...] * inverse_rms).astype(jnp.bfloat16).astype(jnp.float32)
            nxt[item] = (hbuf[item, :, col_ds(c)].astype(jnp.float32) + product).astype(
                jnp.bfloat16
            )
            for r in range(cuts):
                f_along(item, target_item, r).start()

        to_own(item, slot, m).start()
        for k in range(1, dps):
            to_dp(item, slot, m, k).start()
        return carry

    lax.fori_loop(0, items, f_step, 0)

    def b_along(item, target_item):
        return remote(
            dnext.at[item],
            dcol.at[target_item],
            b1_send.at[item],
            b1_recv.at[target_item],
            where(before, c, d),
        )

    def reduce_copy(item, k):
        return remote(
            psend.at[item, k],
            rbuf.at[item, k - 1],
            rs_send.at[item, k - 1],
            rs_recv.at[item, k - 1],
            where(p, peer_of(c, k), d),
        )

    def inner_copy(item, k):
        return remote(
            isend.at[item],
            irecv.at[item, k - 1],
            is_send.at[item, k - 1],
            is_recv.at[item, k - 1],
            where(p, peer_of(c, k), d),
        )

    def b_step(item, carry):
        slot = slots - 1 - item // micro
        m = lax.rem(item, micro)
        layer = slot * pipes + p
        target_item = item + micro * (1 - (p + pipes - 1) // pipes)
        stored = slot * micro + m

        @pl.when(layer == layers - 1)
        def _():
            opening_wait(cot_ref, dcol, item)

        @pl.when(layer < layers - 1)
        def _():
            b_along(item, item).wait_recv()

        @pl.when(layer == 0)
        def _():
            for share in d_shares(item, slot, m):
                share.start()

        d_own(item, slot, m).start()

        @pl.when(layer > 0)
        def _():
            columns = dcol[item]
            inner = jnp.zeros((group, 1), jnp.float32)
            for k in (3, 2, 1, 0):
                cc = peer_of(c, k)
                term = lax.dot_general(
                    columns,
                    w[slot, col_ds(cc), :],
                    (((1,), (1,)), ((), ())),
                    preferred_element_type=jnp.float32,
                ).astype(jnp.bfloat16)
                psend[item, k] = term
                if k:
                    reduce_copy(item, k).start()
                scaled = g_ref[slot, :, col_ds(cc)] * term.astype(jnp.float32)
                hidden = hbuf[stored, :, col_ds(cc)].astype(jnp.float32)
                inner += jnp.sum(hidden * scaled, axis=-1, keepdims=True)
            lanes = jnp.broadcast_to(inner, (group, 128))
            square = jnp.concatenate([lanes] * (128 // group), axis=0)
            isend[item] = jnp.transpose(square)[:8]
            for k in range(tensors - 1, 0, -1):
                inner_copy(item, k).start()

            for k in range(1, tensors):
                inner_copy(item, k).wait_recv()
            sums = isend[item]
            for k in range(1, tensors):
                sums += irecv[item, k - 1]
            inner_all = jnp.transpose(jnp.concatenate([sums] * 16, axis=0))[:group, :1]
            for k in (1, 2, 3):
                reduce_copy(item, k).wait_recv()
            back = psend[item, 0].astype(jnp.float32)
            for k in range(1, tensors):
                back += rbuf[item, k - 1].astype(jnp.float32)
            inverse_rms = rms[stored][:, :1]
            factor = inverse_rms * inverse_rms * inverse_rms * (inner_all * (1.0 / width))
            dnext[item] = (
                dcol[item].astype(jnp.float32)
                + inverse_rms * (g_ref[slot, :, col_ds(c)] * back)
                - factor * hbuf[stored, :, col_ds(c)].astype(jnp.float32)
            ).astype(jnp.bfloat16)
            b_along(item, target_item).start()

        @pl.when((layer > 0) & (m == micro - 1))
        def _():
            for q in range(micro):
                for share in d_shares(item - (micro - 1) + q, slot, q):
                    share.start()

        return carry

    lax.fori_loop(0, items, b_step, 0)

    @pl.when(p == 0)
    def _():
        for m in range(micro):
            for k in range(1, tensors):
                opening(x_ref, hbuf, m, k).wait_send()

    @pl.when(p == pipes - 1)
    def _():
        for m in range(micro):
            for k in range(1, tensors):
                opening(cot_ref, dcol, m, k).wait_send()

    def ending(item, carry):
        f_slot = item // micro
        b_slot = slots - 1 - item // micro
        m = lax.rem(item, micro)
        f_layer = f_slot * pipes + p
        b_layer = b_slot * pipes + p

        @pl.when(f_layer > 0)
        def _():
            for part in range(3):
                for r in range(cuts):
                    spread(item, part, r).wait_send()

        @pl.when(f_layer < layers - 1)
        def _():
            for r in range(cuts):
                f_along(item, item, r).wait_send()

        @pl.when(b_layer > 0)
        def _():
            b_along(item, item).wait_send()
            for k in range(1, tensors):
                reduce_copy(item, k).wait_send()
                inner_copy(item, k).wait_send()

        to_own(item, f_slot, m).wait()
        d_own(item, b_slot, m).wait()
        for k in range(1, dps):
            to_dp(item, f_slot, m, k).wait()
        for share in d_shares(item, b_slot, m):
            share.wait()
        return carry

    lax.fori_loop(0, items, ending, 0)


def chain(inputs, weights, norm_gains, cotangent):
    micro, rows, width = inputs.shape
    slots = weights.shape[0]
    quarter = weights.shape[3]
    pipes = lax.axis_size("pipe")
    tensors = lax.axis_size("tensor")
    dps = lax.axis_size("dp")
    items = slots * micro
    group = tensors * rows
    cuts = 4
    dims = (micro, slots, rows, width, quarter, pipes, tensors, dps, cuts)
    vmem = pl.BlockSpec(memory_space=pltpu.VMEM)
    hbm = pl.BlockSpec(memory_space=pl.ANY)
    dma = pltpu.SemaphoreType.DMA
    out = jax.ShapeDtypeStruct((slots, dps, micro, group, width), jnp.bfloat16)
    return pl.pallas_call(
        functools.partial(chain_kernel, dims),
        out_shape=(out, out),
        in_specs=[vmem, hbm, vmem, vmem],
        out_specs=(hbm, hbm),
        scratch_shapes=[
            pltpu.VMEM((slots, width, quarter), jnp.bfloat16),
            pltpu.VMEM((items, group, width), jnp.bfloat16),
            pltpu.VMEM((items, group, quarter), jnp.bfloat16),
            pltpu.VMEM((items, group, 128), jnp.float32),
            pltpu.VMEM((group, quarter), jnp.float32),
            pltpu.VMEM((items, group, quarter), jnp.bfloat16),
            pltpu.VMEM((items, tensors, group, quarter), jnp.bfloat16),
            pltpu.VMEM((items, tensors - 1, group, quarter), jnp.bfloat16),
            pltpu.VMEM((items, group, quarter), jnp.bfloat16),
            pltpu.VMEM((items, 8, 128), jnp.float32),
            pltpu.VMEM((items, tensors - 1, 8, 128), jnp.float32),
            dma((slots,)),
            dma((micro,)),
            dma((micro, tensors - 1)),
            dma((micro, tensors - 1)),
            dma((items, cuts)),
            dma((items, cuts)),
            dma((items, 3, cuts)),
            dma((items, 3, cuts)),
            dma((items,)),
            dma((items,)),
            dma((items, tensors - 1)),
            dma((items, tensors - 1)),
            dma((items, tensors - 1)),
            dma((items, tensors - 1)),
            dma((items, dps - 1)),
            dma((items, dps - 1)),
            dma((items, dps, tensors)),
            dma((items, dps, tensors)),
            dma((2, items)),
        ],
        compiler_params=pltpu.CompilerParams(
            collective_id=0, has_side_effects=True, vmem_limit_bytes=56 * 1024 * 1024
        ),
        name="chain",
    )(inputs, weights, norm_gains, cotangent)


def body(inputs, weights, norm_gains, cotangent):
    micro, rows, width = inputs.shape
    slots = weights.shape[0]
    quarter = weights.shape[3]
    tensors = lax.axis_size("tensor")
    dps = lax.axis_size("dp")
    own_rows = quarter // dps
    tokens = micro * rows * tensors * dps
    scale = 1.0 / tokens
    h_all, d_all = chain(inputs, weights, norm_gains, cotangent)
    base = (lax.axis_index("tensor") * dps + lax.axis_index("dp")) * own_rows
    h_all = h_all.reshape(slots, tokens, width)
    d_all = d_all.reshape(slots, tokens, width)
    wide = h_all.astype(jnp.float32)
    inverse_rms = lax.rsqrt(jnp.mean(wide * wide, axis=-1, keepdims=True) + EPSILON)
    normed = (wide * inverse_rms * norm_gains).astype(jnp.bfloat16)

    def factor(block):
        parts = []
        for s in range(slots):
            columns = lax.dynamic_slice_in_dim(block[s], base, own_rows, 1)
            gram = lax.dot_general(
                columns, block[s], (((0,), (0,)), ((), ())), preferred_element_type=jnp.float32
            )
            parts.append((gram * scale).astype(jnp.bfloat16))
        return jnp.stack(parts, 1)[:, :, None, :]

    return factor(normed), factor(d_all)


def solution(mesh):
    in_specs = (
        P(None, ("tensor", "dp"), None),
        P(None, "pipe", None, "tensor"),
        P(None, "pipe", None),
        P(None, ("tensor", "dp"), None),
    )
    out_specs = (P(("tensor", "dp"), None, "pipe", None), P(("tensor", "dp"), None, "pipe", None))
    return jax.shard_map(body, mesh=mesh, in_specs=in_specs, out_specs=out_specs, check_vma=False)
```

time: 332 us -> 279 us (0.84); the launches traced: 332 us -> 276 us
  Pallas kernels: 262 us -> 205 us
    pallas_call x1, Pallas kernels: 262 us -> 205 us  [chain(): pl.pallas_call(functools.partial(chain_kernel, dims), out_shape=(out, out...]
where the time goes in v2:
time: 279 us; the launch traced here: 276 us
  Pallas kernels  205 us (73%)
  local copies, waits for them, and re-layouts  39.9 us (14%)
  other arithmetic  18.6 us (7%)
  matrix products  11.1 us (4%)
    pallas_call x1, Pallas kernels, chain(): pl.pallas_call(functools.partial(chain_kernel, dims), out_shape=(out, out...  205 us
    unnamed x9, local copies, waits for them, and re-layouts  34.1 us
    broadcast_in_dim x2, other arithmetic, factor(): return jnp.stack(parts, 1)[:, :, None, :]  13.8 us
    dot_general x4, matrix products, factor(): lax.dot_general(columns, block[s], (((0,), (0,)), ((), ())), preferred_el...  11.1 us
    slice x2, local copies, waits for them, and re-layouts, factor(): columns = lax.dynamic_slice_in_dim(block[s], base, own_rows, 1)  5.73 us

profile of v2, /device:TPU:0, one launch (start us, length us, event | category | flops | bytes accessed | tf_op | source)
XLA Modules:
  0.0 275.5 jit_solution(16057905589138799468)
XLA Ops:
  0.6 0.8 copy.10
  1.4 205.2 %chain.1 = (bf16[2,2,2,64,4096]{4,3,2,1,0:T(8,128)(2,1)}, bf16[2,2,2,64,4096]{4,3,2,1,0:T(8,128)(2,1)}) custom-call(bf16[2,16,4096]{2,1,0:T(8,128)(2,1)} %x_ref.1, bf16[2,1,4096,1024]{3,2,1,0:T(8,128)(2,1)} %w_hbm.1, f32[2,1,4096]{2,1,0:T(1,128)} %g_ref.1, bf16[2,16,4096]{2,1,0:T(8,128)(2,1)} %cot_ref.1), custom_call_target="tpu_custom_call" | custom-call | tf_op jit(solution)/shard_map/chain/pallas_call | solution.py:434
  206.6 0.0 copy-start
  206.7 4.1 %fusion.18 = (bf16[1,2,2,64,4096]{4,3,2,1,0:T(8,128)(2,1)S(1)}, bf16[1,2,2,64,4096]{4,3,2,1,0:T(8,128)(2,1)}) fusion(bf16[2,2,2,64,4096]{4,3,2,1,0:T(8,128)(2,1)} %get-tuple-element.5), kind=kLoop, calls=%fused_computation.28 | loop fusion | bytes 8388608 | tf_op jit(solution)/shard_map/slice | solution.py:498
  210.7 0.0 copy-done
  210.7 0.9 multiply_reduce_fusion
  211.6 0.1 rsqrt.12
  211.7 3.8 %fusion.1 = bf16[2,256,4096]{2,1,0:T(8,128)(2,1)S(1)} fusion(f32[2,4096]{1,0:T(2,128)S(1)} %bitcast.39, f32[2,256]{1,0:T(2,128)S(1)} %rsqrt.12, bf16[2,2,2,64,4096]{4,3,2,1,0:T(8,128)(2,1)} %get-tuple-element.4), kind=kLoop, calls=%fused_computation.4 | loop fusion | flops 8388608 | bytes 8423424 | tf_op jit(solution)/shard_map/convert_element_type | solution.py:493
  215.6 1.7 fusion.19
  217.2 0.0 copy-start.1
  217.2 1.3 fusion.2
  218.5 0.3 copy-done.1
  218.8 3.3 %fusion.5 = bf16[512,1,4096]{2,0,1:T(8,128)(2,1)} fusion(bf16[256,4096]{1,0:T(8,128)(2,1)S(1)} %bitcast.38, s32[]{:T(128)S(6)} %select_n.2), kind=kOutput, calls=%fused_computation.13 | convolution fusion | flops 1077936128 | bytes 6553604 | tf_op jit(solution)/shard_map/dot_general | solution.py:499
  222.1 3.2 %fusion.4 = bf16[512,1,4096]{2,0,1:T(8,128)(2,1)} fusion(bf16[256,4096]{1,0:T(8,128)(2,1)S(1)} %bitcast.37, s32[]{:T(128)S(6)} %select_n.2), kind=kOutput, calls=%fused_computation.12 | convolution fusion | flops 1077936128 | bytes 6553604 | tf_op jit(solution)/shard_map/dot_general | solution.py:499
  225.4 7.6 %maximum_bitcast_fusion.1 = bf16[512,2,1,4096]{3,0,1,2:T(8,128)(2,1)} fusion(bf16[512,1,4096]{2,0,1:T(8,128)(2,1)} %fusion.5, bf16[512,1,4096]{2,0,1:T(8,128)(2,1)} %fusion.4), kind=kLoop, calls=%fused_computation.1 | loop fusion | flops 4194304 | bytes 16777216 | tf_op jit(solution)/shard_map/broadcast_in_dim | solution.py:503
  233.0 0.0 copy-start.2
  233.0 16.7 %copy.7 = bf16[512,2,1,4096]{3,1,2,0:T(2,128)(2,1)} copy(bf16[512,2,1,4096]{3,0,1,2:T(8,128)(2,1)} %maximum_bitcast_fusion.1) | data formatting | bytes 16777216
  249.7 0.0 copy-done.2
  249.7 3.3 %fusion.3 = bf16[512,1,4096]{2,0,1:T(8,128)(2,1)} fusion(bf16[1,256,4096]{2,1,0:T(8,128)(2,1)S(1)} %copy-done.2, s32[]{:T(128)S(6)} %select_n.2), kind=kOutput, calls=%fused_computation.11 | convolution fusion | flops 1077936128 | bytes 6553604 | tf_op jit(solution)/shard_map/dot_general | solution.py:499
  253.0 6.2 %maximum_bitcast_fusion = bf16[512,2,1,4096]{3,0,1,2:T(8,128)(2,1)} fusion(bf16[512,1,4096]{2,0,1:T(8,128)(2,1)} %fusion.3, bf16[512,1,4096]{2,0,1:T(8,128)(2,1)S(1)} %fusion.2), kind=kLoop, calls=%fused_computation | loop fusion | flops 4194304 | bytes 16777216 | tf_op jit(solution)/shard_map/broadcast_in_dim | solution.py:503
  259.2 16.4 %copy.6 = bf16[512,2,1,4096]{3,1,2,0:T(2,128)(2,1)} copy(bf16[512,2,1,4096]{3,0,1,2:T(8,128)(2,1)} %maximum_bitcast_fusion) | data formatting | bytes 16777216
  (1 shorter events, 0.0 us)
Async XLA Ops:
  206.6 4.1 %copy-start = (bf16[2,2,2,64,4096]{4,3,2,1,0:T(8,128)(2,1)S(1)}, bf16[2,2,2,64,4096]{4,3,2,1,0:T(8,128)(2,1)}, u32[]{:S(2)}) copy-start(bf16[2,2,2,64,4096]{4,3,2,1,0:T(8,128)(2,1)} %get-tuple-element.4) | copy-start | bytes 12582916
  217.2 1.6 copy-start.1
  233.0 16.7 %copy-start.2 = (bf16[1,256,4096]{2,1,0:T(8,128)(2,1)S(1)}, bf16[1,256,4096]{2,1,0:T(8,128)(2,1)}, u32[]{:S(2)}) copy-start(bf16[1,256,4096]{2,1,0:T(8,128)(2,1)} %get-tuple-element.11) | copy-start | bytes 6291460

commit v3 on v2

--- a/solution.py
+++ b/solution.py
@@ -475,6 +475,65 @@
     )(inputs, weights, norm_gains, cotangent)
 
 
+def gram_kernel(base_rows, scale, normalized, x_ref, g_ref, out_ref, full, mixed):
+    slots, tokens, width = x_ref.shape
+    block = out_ref.shape[0]
+    step = pl.program_id(0)
+
+    if normalized:
+
+        @pl.when(step == 0)
+        def _():
+            for s in range(slots):
+                for t in range(0, tokens, 32):
+                    wide = x_ref[s, t : t + 32].astype(jnp.float32)
+                    mean = jnp.mean(wide * wide, axis=-1, keepdims=True)
+                    inverse_rms = lax.rsqrt(mean + EPSILON)
+                    full[s, t : t + 32] = (wide * inverse_rms * g_ref[s]).astype(jnp.bfloat16)
+
+    source = full if normalized else x_ref
+    own = (lax.axis_index("tensor") * lax.axis_size("dp") + lax.axis_index("dp")) * base_rows
+    start = pl.multiple_of(own + step * block, block)
+    columns = [source[s, :, pl.ds(start, block)] for s in range(slots)]
+    span = 512
+    for n in range(width // span):
+        cut = slice(n * span, (n + 1) * span)
+        for s in range(slots):
+            gram = lax.dot_general(
+                columns[s],
+                source[s, :, cut],
+                (((0,), (0,)), ((), ())),
+                preferred_element_type=jnp.float32,
+            )
+            for q in range(span // 128):
+                mixed[q, pl.ds(s, block, slots), :] = gram[:, q * 128 : (q + 1) * 128] * scale
+        for q in range(span // 128):
+            lane = slice(n * span + q * 128, n * span + (q + 1) * 128)
+            out_ref[:, :, lane] = mixed[q].astype(jnp.bfloat16).reshape(block, slots, 128)
+
+
+def gram_call(block, gains, own_rows, normalized):
+    slots, tokens, width = block.shape
+    tile = min(128, own_rows)
+    out = pl.pallas_call(
+        functools.partial(gram_kernel, own_rows, 1.0 / tokens, normalized),
+        grid=(own_rows // tile,),
+        out_shape=jax.ShapeDtypeStruct((own_rows, slots, width), jnp.bfloat16),
+        in_specs=[
+            pl.BlockSpec(block.shape, lambda i: (0, 0, 0), pipeline_mode=pl.Buffered(1)),
+            pl.BlockSpec(gains.shape, lambda i: (0, 0, 0), pipeline_mode=pl.Buffered(1)),
+        ],
+        out_specs=pl.BlockSpec((tile, slots, width), lambda i: (i, 0, 0)),
+        scratch_shapes=[
+            pltpu.VMEM((slots, tokens, width) if normalized else (slots, 8, 128), jnp.bfloat16),
+            pltpu.VMEM((4, tile * slots, 128), jnp.float32),
+        ],
+        compiler_params=pltpu.CompilerParams(vmem_limit_bytes=min(62 << 20, (32 << 20) + 8 * block.size)),
+        name="gram",
+    )(block, gains)
+    return out.reshape(own_rows, slots, 1, width)
+
+
 def body(inputs, weights, norm_gains, cotangent):
     micro, rows, width = inputs.shape
     slots = weights.shape[0]
@@ -483,26 +542,11 @@
     dps = lax.axis_size("dp")
     own_rows = quarter // dps
     tokens = micro * rows * tensors * dps
-    scale = 1.0 / tokens
     h_all, d_all = chain(inputs, weights, norm_gains, cotangent)
-    base = (lax.axis_index("tensor") * dps + lax.axis_index("dp")) * own_rows
     h_all = h_all.reshape(slots, tokens, width)
     d_all = d_all.reshape(slots, tokens, width)
-    wide = h_all.astype(jnp.float32)
-    inverse_rms = lax.rsqrt(jnp.mean(wide * wide, axis=-1, keepdims=True) + EPSILON)
-    normed = (wide * inverse_rms * norm_gains).astype(jnp.bfloat16)
-
-    def factor(block):
-        parts = []
-        for s in range(slots):
-            columns = lax.dynamic_slice_in_dim(block[s], base, own_rows, 1)
-            gram = lax.dot_general(
-                columns, block[s], (((0,), (0,)), ((), ())), preferred_element_type=jnp.float32
-            )
-            parts.append((gram * scale).astype(jnp.bfloat16))
-        return jnp.stack(parts, 1)[:, :, None, :]
-
-    return factor(normed), factor(d_all)
+    act = gram_call(h_all, norm_gains, own_rows, True)
+    return act, gram_call(d_all, norm_gains, own_rows, False)
 
 
 def solution(mesh):

time: 279 us -> 234 us (0.84)
  local copies, waits for them, and re-layouts: 39.9 us -> 2.34 us
  Pallas kernels: 205 us -> 228 us
  other arithmetic: 18.6 us -> 0 us
  matrix products: 11.1 us -> 0 us
    unnamed x9 -> x6, local copies, waits for them, and re-layouts: 34.1 us -> 2.34 us
    pallas_call x0 -> x2, Pallas kernels: none -> 22.3 us  [gram_call(): pl.pallas_call(functools.partial(gram_kernel, own_rows, 1.0 / tokens, nor...]
    broadcast_in_dim x2 -> x0, other arithmetic: 13.8 us -> none  [factor(): return jnp.stack(parts, 1)[:, :, None, :]]
    dot_general x4 -> x0, matrix products: 11.1 us -> none  [factor(): lax.dot_general(columns, block[s], (((0,), (0,)), ((), ())), preferred_el...]
    slice x2 -> x0, local copies, waits for them, and re-layouts: 5.73 us -> none  [factor(): columns = lax.dynamic_slice_in_dim(block[s], base, own_rows, 1)]
    convert_element_type x1 -> x0, other arithmetic: 3.84 us -> none  [body(): normed = (wide * inverse_rms * norm_gains).astype(jnp.bfloat16)]
where the time goes in v3:
time: 234 us; the launch traced here: 231 us
  Pallas kernels  228 us (97%)
  local copies, waits for them, and re-layouts  2.34 us (1%)
    pallas_call x1, Pallas kernels, chain(): pl.pallas_call(functools.partial(chain_kernel, dims), out_shape=(out, out...  205 us
    pallas_call x2, Pallas kernels, gram_call(): pl.pallas_call(functools.partial(gram_kernel, own_rows, 1.0 / tokens, nor...  22.3 us

profile of v3, /device:TPU:0, one launch (start us, length us, event | category | flops | bytes accessed | tf_op | source)
XLA Modules:
  0.0 230.5 jit_solution(11105134186560096952)
XLA Ops:
  0.6 0.0 copy-start.2
  0.6 205.2 %chain.1 = (bf16[2,2,2,64,4096]{4,3,2,1,0:T(8,128)(2,1)}, bf16[2,2,2,64,4096]{4,3,2,1,0:T(8,128)(2,1)}) custom-call(bf16[2,16,4096]{2,1,0:T(8,128)(2,1)} %x_ref.1, bf16[2,1,4096,1024]{3,2,1,0:T(8,128)(2,1)} %w_hbm.1, f32[2,1,4096]{2,1,0:T(1,128)} %g_ref.5, bf16[2,16,4096]{2,1,0:T(8,128)(2,1)} %cot_ref.1), custom_call_target="tpu_custom_call" | custom-call | tf_op jit(solution)/shard_map/chain/pallas_call | solution.py:434
  205.9 0.0 copy-start
  205.9 0.0 copy-done.2
  205.9 0.0 copy-start.1
  205.9 2.3 %copy-done.1 = bf16[2,2,2,64,4096]{4,3,2,1,0:T(8,128)(2,1)S(1)} copy-done((bf16[2,2,2,64,4096]{4,3,2,1,0:T(8,128)(2,1)S(1)}, bf16[2,2,2,64,4096]{4,3,2,1,0:T(8,128)(2,1)}, u32[]{:S(2)}) %copy-start.1) | copy-done | bytes 4194328
  208.2 10.0 %gram.3 = bf16[512,2,4096]{2,1,0:T(2,128)(2,1)} custom-call(bf16[2,256,4096]{2,1,0:T(8,128)(2,1)S(1)} %bitcast.9, f32[2,1,4096]{2,1,0:T(1,128)S(1)} %copy-done.2), custom_call_target="tpu_custom_call" | custom-call | tf_op jit(solution)/shard_map/gram/pallas_call | solution.py:518
  218.2 0.0 copy-done
  218.3 12.3 %gram.2 = bf16[512,2,4096]{2,1,0:T(2,128)(2,1)} custom-call(bf16[2,256,4096]{2,1,0:T(8,128)(2,1)S(1)} %bitcast.8, f32[2,1,4096]{2,1,0:T(1,128)S(1)} %copy-done.2), custom_call_target="tpu_custom_call" | custom-call | tf_op jit(solution)/shard_map/gram/pallas_call | solution.py:518
Async XLA Ops:
  0.6 205.2 %copy-start.2 = (f32[2,1,4096]{2,1,0:T(1,128)S(1)}, f32[2,1,4096]{2,1,0:T(1,128)}, u32[]{:S(2)}) copy-start(f32[2,1,4096]{2,1,0:T(1,128)} %g_ref.5) | copy-start | bytes 98308
  205.9 12.4 %copy-start = (bf16[2,2,2,64,4096]{4,3,2,1,0:T(8,128)(2,1)S(1)}, bf16[2,2,2,64,4096]{4,3,2,1,0:T(8,128)(2,1)}, u32[]{:S(2)}) copy-start(bf16[2,2,2,64,4096]{4,3,2,1,0:T(8,128)(2,1)} %get-tuple-element.4) | copy-start | bytes 12582916
  205.9 2.3 %copy-start.1 = (bf16[2,2,2,64,4096]{4,3,2,1,0:T(8,128)(2,1)S(1)}, bf16[2,2,2,64,4096]{4,3,2,1,0:T(8,128)(2,1)}, u32[]{:S(2)}) copy-start(bf16[2,2,2,64,4096]{4,3,2,1,0:T(8,128)(2,1)} %get-tuple-element.5) | copy-start | bytes 12582916
